TPU v7x, 256 devices: a whole 4x4x8 slice. The times are simulated.
256 devices in a mesh: row: 16 (over z, core), col: 16 (over x, y).
Axes of the slice: x: 4, y: 4, z: 8, core: 2. Of those that a mesh axis runs over, the one named last changes fastest.
Arguments:
- token_ids: int32 [32, 256], P('row'), may hold values from 0 to 16383
- passage_lengths: int32 [32], P('row'), may hold values from 64 to 256, as said below
- embedding: bfloat16 [16384, 4096], P(None, 'col'), may hold values from -8 to 8
- attn_gain: bfloat16 [4096], P('col'), may hold values from 0.25 to 1.75
- final_gain: bfloat16 [4096], P('col'), may hold values from 0.25 to 1.75
- query_weight: bfloat16 [4096, 4096], P('row', 'col'), may hold values from -0.5 to 0.5
- key_weight: bfloat16 [4096, 4096], P('row', 'col'), may hold values from -0.5 to 0.5
- value_weight: bfloat16 [4096, 4096], P('row', 'col'), may hold values from -0.09375 to 0.09375
- out_weight: bfloat16 [4096, 4096], P('row', 'col'), may hold values from -0.09375 to 0.09375
- crosskey_weight: bfloat16 [4096, 4096], P('row', 'col'), may hold values from -0.09375 to 0.09375
- crossvalue_weight: bfloat16 [4096, 4096], P('row', 'col'), may hold values from -0.09375 to 0.09375
Outputs:
- hidden_out: bfloat16 [8192, 4096], P('row', 'col')
- cross_keys: bfloat16 [8192, 16, 256], P('row', 'col')
- cross_values: bfloat16 [8192, 16, 256], P('row', 'col')
Inputs may be any that keep to these rules, and one draw needn't show every extreme that they name: `passage_lengths`: some passage of every draw has all 256 slots valid.
All inputs are finite; a program needn't handle non-finite values.
Results may differ from a plain program's by a relative error of at most 0.0082.
Values may be sent and summed in bfloat16 or wider, within the bound.
No kernel may reach another device: no remote copies, remote signals or barrier semaphores. Data moves between devices by JAX's collectives and lax.ppermute only.
A program may use at most 64 MiB of HBM per device.

v0:
```python
import jax
import jax.numpy as jnp
from jax import lax
from jax.sharding import PartitionSpec as P

D = 4096
HD = 256
PLEN = 256
epsilon = 1e-06
masked_score = -1000000000.0


def scaled_rows(widened, summed, gain_row):
    inverse = lax.rsqrt(summed / D + epsilon)
    return (widened * inverse * gain_row.astype(jnp.float32)).astype(jnp.bfloat16)


def spread_norm(row_block, gain_row, which):
    widened = row_block.astype(jnp.float32)
    partial_sum = jnp.sum(widened * widened, axis=1, keepdims=True)
    if which == 0:
        summed = lax.psum(partial_sum, "col")
        return lax.all_gather(
            scaled_rows(widened, summed, gain_row[None, :]), "col", axis=1, tiled=True
        )
    else:
        summed = lax.psum(partial_sum, "col")
        return lax.all_gather(
            scaled_rows(widened, summed, gain_row[None, :]), "col", axis=1, tiled=True
        )


def add_terms(source, pieces):
    return tuple(
        (
            jnp.dot(source, weight_piece, preferred_element_type=jnp.float32)
            for weight_piece in pieces
        )
    )


def attend(query_rows, key_rows, value_rows, passage_lengths):
    tok_rows, local_width = query_rows.shape
    passages_here = tok_rows // PLEN
    heads_here = local_width // HD
    query_four = query_rows.reshape(passages_here, PLEN, heads_here, HD)
    key_four = key_rows.reshape(passages_here, PLEN, heads_here, HD)
    value_four = value_rows.reshape(passages_here, PLEN, heads_here, HD)
    scores = jnp.einsum(
        "pihd,pjhd->phij", query_four, key_four, preferred_element_type=jnp.float32
    ) * HD ** (-0.5)
    valid = jnp.arange(PLEN, dtype=jnp.int32)[None, :] < passage_lengths[:, None]
    scores = jnp.where(valid[:, None, None, :], scores, masked_score)
    highest = jnp.max(scores, axis=-1, keepdims=True)
    expon = jnp.exp(scores - highest)
    probs = (expon / jnp.sum(expon, axis=-1, keepdims=True)).astype(jnp.bfloat16)
    mixed = jnp.einsum("phij,pjhd->pihd", probs, value_four, preferred_element_type=jnp.float32)
    return mixed.astype(jnp.bfloat16).reshape(tok_rows, local_width)


def shards(
    token_ids,
    passage_lengths,
    embedding,
    attn_gain,
    final_gain,
    query_weight,
    key_weight,
    value_weight,
    out_weight,
    crosskey_weight,
    crossvalue_weight,
):
    embedded = jnp.take(embedding, token_ids.reshape(-1), axis=0)
    normed = spread_norm(embedded, attn_gain, 0)
    tok_rows = normed.shape[0]
    local_width = query_weight.shape[1]
    query_sum, key_sum, value_sum = add_terms(
        normed,
        (
            lax.all_gather(query_weight, "row", axis=0, tiled=True),
            lax.all_gather(key_weight, "row", axis=0, tiled=True),
            lax.all_gather(value_weight, "row", axis=0, tiled=True),
        ),
    )
    attended = attend(
        query_sum.astype(jnp.bfloat16),
        key_sum.astype(jnp.bfloat16),
        value_sum.astype(jnp.bfloat16),
        passage_lengths,
    )
    heads_full = lax.all_gather(attended, "col", axis=1, tiled=True)
    (projected,) = add_terms(heads_full, (lax.all_gather(out_weight, "row", axis=0, tiled=True),))
    hidden_out = (embedded.astype(jnp.float32) + projected).astype(jnp.bfloat16)
    final_normed = spread_norm(hidden_out, final_gain, 1)
    crosskey_sum, crossvalue_sum = add_terms(
        final_normed,
        (
            lax.all_gather(crosskey_weight, "row", axis=0, tiled=True),
            lax.all_gather(crossvalue_weight, "row", axis=0, tiled=True),
        ),
    )
    heads_here = local_width // HD
    cross_keys = crosskey_sum.astype(jnp.bfloat16).reshape(tok_rows, heads_here, HD)
    cross_values = crossvalue_sum.astype(jnp.bfloat16).reshape(tok_rows, heads_here, HD)
    return (hidden_out, cross_keys, cross_values)


def solution(mesh):
    return jax.shard_map(
        shards,
        mesh=mesh,
        in_specs=(
            P("row", None),
            P("row"),
            P(None, "col"),
            P("col"),
            P("col"),
            P("row", "col"),
            P("row", "col"),
            P("row", "col"),
            P("row", "col"),
            P("row", "col"),
            P("row", "col"),
        ),
        out_specs=(P("row", "col"), P("row", "col", None), P("row", "col", None)),
        check_vma=False,
    )
```

profile of v0, /device:TPU:1, one launch (start us, length us, event | category | flops | bytes accessed | tf_op | source)
XLA Modules:
  0.0 447.0 jit_solution(17359749313425114075)
XLA Ops:
  7.2 0.0 copy-start
  7.2 0.0 all-gather.14.cloned.1.call-start
  7.2 0.7 all-gather.14.cloned.1.call-update
  7.9 0.0 all-gather.10.cloned.1.call-start
  8.0 0.7 convert_element_type.53
  8.6 0.7 copy.22
  9.3 0.0 copy-start.1
  9.3 6.0 %gather_fusion = bf16[512,256]{1,0:T(8,128)(2,1)S(1)} fusion(bf16[16384,256]{1,0:T(8,128)(2,1)} %param.13, s32[1024]{0:T(1024)S(1)} %pad_clamp_fusion), kind=kCustom, calls=%fused_computation | custom fusion | bytes 526336 | tf_op jit(solution)/shard_map/jit(_take)/gather | solution.py:74
  15.4 0.1 copy.17
  15.5 0.0 copy-done
  15.5 0.1 fusion.10
  15.6 34.2 %psum.14 = f32[512,1]{0,1:T(1,128)S(1)} all-reduce(f32[512,1]{0,1:T(1,128)S(1)} %bitcast.48), channel_id=1, replica_groups=mesh['row'=16,'col'=16] {'col'}, use_global_device_ids=true, to_apply=%region_1.2 | all-reduce | flops 512 | bytes 4096 | tf_op jit(solution)/shard_map/psum | solution.py:22
  49.9 0.8 fusion.12
  50.7 0.0 all-gather.10.cloned.1.call-update
  50.7 0.0 all-gather.16.cloned.1.call-start
  50.8 0.7 all-gather.16.cloned.1.call-update
  51.5 0.0 all-gather.12.cloned.1.call-start
  51.5 0.5 all-gather.12.cloned.1.call-update
  52.0 0.0 all-gather.20.cloned.1.call-start
  52.1 0.5 all-gather.20.cloned.1.call-update
  52.6 0.0 all-gather.18.cloned.1.call-start
  52.7 0.0 copy-done.1
  52.7 0.1 iota_compare_fusion
  52.8 0.7 all-gather.14.cloned.1.call-done
  53.5 58.8 %all-gather.10.cloned.1.call-done = bf16[512,4096]{0,1:T(8,128)(2,1)} async-done(((bf16[512,256]{0,1:T(8,128)(2,1)}), bf16[512,4096]{0,1:T(8,128)(2,1)}) %all-gather.10.cloned.1.call-update) | async-done | bytes 4194320 | tf_op jit(solution)/shard_map/all_gather | solution.py:23
  112.3 4.2 convolution_convert_fusion.4
  116.4 37.4 %all-gather.16.cloned.1.call-done = bf16[4096,256]{1,0:T(8,128)(2,1)} async-done(((bf16[256,256]{1,0:T(8,128)(2,1)}), bf16[4096,256]{1,0:T(8,128)(2,1)}) %all-gather.16.cloned.1.call-update) | async-done | bytes 2097168 | tf_op jit(solution)/shard_map/all_gather | solution.py:82
  153.9 4.2 convolution_convert_fusion.3
  158.0 0.4 fusion.15
  158.4 0.3 fusion.3
  158.7 34.7 %all-gather.12.cloned.1.call-done = bf16[4096,256]{1,0:T(8,128)(2,1)} async-done(((bf16[256,256]{1,0:T(8,128)(2,1)}), bf16[4096,256]{1,0:T(8,128)(2,1)}) %all-gather.12.cloned.1.call-update) | async-done | bytes 2097168 | tf_op jit(solution)/shard_map/all_gather | solution.py:83
  193.4 4.2 convolution_convert_fusion.5
  197.6 0.0 copy-start.2
  197.6 1.0 convolution_convert_fusion.2
  198.6 0.0 all-gather.18.cloned.1.call-update
  198.6 0.0 all-gather.24.cloned.1.call-start
  198.7 0.7 all-gather.24.cloned.1.call-update
  199.4 0.0 all-gather.22.cloned.1.call-start
  199.4 0.0 copy-done.2
  199.5 33.5 %all-gather.20.cloned.1.call-done = bf16[4096,256]{1,0:T(8,128)(2,1)} async-done(((bf16[256,256]{1,0:T(8,128)(2,1)}), bf16[4096,256]{1,0:T(8,128)(2,1)}) %all-gather.20.cloned.1.call-update) | async-done | bytes 2097168 | tf_op jit(solution)/shard_map/all_gather | solution.py:93
  232.9 61.3 %all-gather.18.cloned.1.call-done = bf16[512,4096]{1,0:T(8,128)(2,1)} async-done(((bf16[512,256]{1,0:T(8,128)(2,1)}), bf16[512,4096]{1,0:T(8,128)(2,1)}) %all-gather.18.cloned.1.call-update) | async-done | bytes 4194320 | tf_op jit(solution)/shard_map/all_gather | solution.py:92
  294.2 4.2 fusion.7
  298.4 31.3 %psum.15 = f32[512,1]{0,1:T(1,128)S(1)} all-reduce(f32[512,1]{0,1:T(1,128)S(1)} %bitcast.54), channel_id=1, replica_groups=mesh['row'=16,'col'=16] {'col'}, use_global_device_ids=true, to_apply=%region_5.6 | all-reduce | flops 512 | bytes 4096 | tf_op jit(solution)/shard_map/psum | solution.py:27
  329.7 0.8 fusion.9
  330.5 0.0 all-gather.22.cloned.1.call-update
  330.5 0.0 all-gather.26.cloned.1.call-start
  330.6 0.7 all-gather.26.cloned.1.call-update
  331.3 0.8 copy.19
  332.1 4.6 %all-gather.24.cloned.1.call-done = bf16[4096,256]{1,0:T(8,128)(2,1)} async-done(((bf16[256,256]{1,0:T(8,128)(2,1)}), bf16[4096,256]{1,0:T(8,128)(2,1)}) %all-gather.24.cloned.1.call-update) | async-done | bytes 2097168 | tf_op jit(solution)/shard_map/all_gather | solution.py:99
  336.7 57.3 %all-gather.22.cloned.1.call-done = bf16[512,4096]{0,1:T(8,128)(2,1)} async-done(((bf16[512,256]{0,1:T(8,128)(2,1)}), bf16[512,4096]{0,1:T(8,128)(2,1)}) %all-gather.22.cloned.1.call-update) | async-done | bytes 4194320 | tf_op jit(solution)/shard_map/all_gather | solution.py:28
  394.0 4.9 %fusion.5 = bf16[512,1,256]{2,0,1:T(8,128)(2,1)} fusion(bf16[512,4096]{0,1:T(8,128)(2,1)} %all-gather.22.cloned.1.call-done, bf16[4096,256]{1,0:T(8,128)(2,1)} %all-gather.24.cloned.1.call-done), kind=kOutput, calls=%fused_computation.14 | convolution fusion | flops 1073872896 | bytes 6553600 | tf_op jit(solution)/shard_map/dot_general | solution.py:36
  398.8 36.7 %all-gather.26.cloned.1.call-done = bf16[4096,256]{1,0:T(8,128)(2,1)} async-done(((bf16[256,256]{1,0:T(8,128)(2,1)}), bf16[4096,256]{1,0:T(8,128)(2,1)}) %all-gather.26.cloned.1.call-update) | async-done | bytes 2097168 | tf_op jit(solution)/shard_map/all_gather | solution.py:100
  435.6 4.9 %fusion.6 = bf16[512,1,256]{2,0,1:T(8,128)(2,1)} fusion(bf16[512,4096]{0,1:T(8,128)(2,1)} %all-gather.22.cloned.1.call-done, bf16[4096,256]{1,0:T(8,128)(2,1)} %all-gather.26.cloned.1.call-done), kind=kOutput, calls=%fused_computation.15 | convolution fusion | flops 1073872896 | bytes 6553600 | tf_op jit(solution)/shard_map/dot_general | solution.py:36
  (7 shorter events, 0.1 us)
Async XLA Ops:
  7.2 8.3 %copy-start = (s32[2,256]{1,0:T(2,128)S(1)}, s32[2,256]{1,0:T(2,128)}, u32[]{:S(2)}) copy-start(s32[2,256]{1,0:T(2,128)} %param.11) | copy-start | bytes 6148
  7.2 46.3 %all-gather.14.cloned.1.call-start = ((), (), s32[]{:S(2)}) async-start(), calls=%async_computation.2 | async-start | bytes 2228224 | tf_op jit(solution)/shard_map/all_gather | solution.py:81
  7.9 104.3 %all-gather.10.cloned.1.call-start = ((), (), s32[]{:S(2)}) async-start(), calls=%async_computation | async-start | bytes 4456448 | tf_op jit(solution)/shard_map/all_gather | solution.py:23
  9.3 43.4 %copy-start.1 = (s32[2]{0:T(128)S(1)}, s32[2]{0:T(128)}, u32[]{:S(2)}) copy-start(s32[2]{0:T(128)} %param.12) | copy-start | bytes 28
  50.7 103.1 %all-gather.16.cloned.1.call-start = ((), (), s32[]{:S(2)}) async-start(), calls=%async_computation.3 | async-start | bytes 2228224 | tf_op jit(solution)/shard_map/all_gather | solution.py:82
  51.5 141.9 %all-gather.12.cloned.1.call-start = ((), (), s32[]{:S(2)}) async-start(), calls=%async_computation.1 | async-start | bytes 2228224 | tf_op jit(solution)/shard_map/all_gather | solution.py:83
  52.0 180.9 %all-gather.20.cloned.1.call-start = ((), (), s32[]{:S(2)}) async-start(), calls=%async_computation.5 | async-start | bytes 2228224 | tf_op jit(solution)/shard_map/all_gather | solution.py:93
  52.6 241.6 %all-gather.18.cloned.1.call-start = ((), (), s32[]{:S(2)}) async-start(), calls=%async_computation.4 | async-start | bytes 4456448 | tf_op jit(solution)/shard_map/all_gather | solution.py:92
  197.6 1.9 copy-start.2
  198.6 138.1 %all-gather.24.cloned.1.call-start = ((), (), s32[]{:S(2)}) async-start(), calls=%async_computation.7 | async-start | bytes 2228224 | tf_op jit(solution)/shard_map/all_gather | solution.py:99
  199.4 194.6 %all-gather.22.cloned.1.call-start = ((), (), s32[]{:S(2)}) async-start(), calls=%async_computation.6 | async-start | bytes 4456448 | tf_op jit(solution)/shard_map/all_gather | solution.py:28
  330.5 105.1 %all-gather.26.cloned.1.call-start = ((), (), s32[]{:S(2)}) async-start(), calls=%async_computation.8 | async-start | bytes 2228224 | tf_op jit(solution)/shard_map/all_gather | solution.py:100
Sparse Core Ops, SparseCore 0:
  9.8 43.6 all-gather.13
  56.5 55.7 all-gather.9
  114.1 39.7 all-gather.15
  155.5 37.8 all-gather.11
  195.1 37.8 all-gather.19
  235.7 58.4 all-gather.17
  296.0 40.6 all-gather.23
  339.7 54.2 all-gather.21
  395.8 39.7 all-gather.25
where the time goes:
time: 447 us
  waiting for transfers between devices  329 us (74%)
  blocking collectives  65.5 us (15%)
  matrix products  28.1 us (6%)
  between operations  14 us (3%)
  local copies, waits for them, and re-layouts  7.71 us (2%)
    all_gather x2, waiting for transfers between devices, spread_norm(): lax.all_gather(scaled_rows(widened, summed, gain_row[None, :]), 'col', ax...  116 us
    psum x2, blocking collectives, spread_norm(): summed = lax.psum(partial_sum, 'col')  65.5 us
    all_gather x1, waiting for transfers between devices, shards(): heads_full = lax.all_gather(attended, 'col', axis=1, tiled=True)  61.3 us
    all_gather x1, waiting for transfers between devices, shards(): lax.all_gather(key_weight, 'row', axis=0, tiled=True)  37.4 us
    all_gather x1, waiting for transfers between devices, shards(): lax.all_gather(crossvalue_weight, 'row', axis=0, tiled=True)  36.7 us
    all_gather x1, waiting for transfers between devices, shards(): lax.all_gather(value_weight, 'row', axis=0, tiled=True)  34.7 us
    all_gather x1, waiting for transfers between devices, shards(): lax.all_gather(out_weight, 'row', axis=0, tiled=True)  33.5 us
    dot_general x6, matrix products, add_terms(): jnp.dot(source, weight_piece, preferred_element_type=jnp.float32)  26.4 us
  transfers between devices with their start and end apart: 9, of which 9 were waited for; matrix products, arithmetic and copies ran while one was open for 7% of the time, Pallas kernels for 0%

commit v1 on v0

--- a/solution.py
+++ b/solution.py
@@ -10,6 +10,13 @@
 masked_score = -1000000000.0
 
 
+def all_by_exchange(block, axis, d):
+    size = lax.axis_size(axis)
+    blocks = jnp.stack([block for _ in range(size)])
+    blocks = lax.all_to_all(blocks, axis, split_axis=0, concat_axis=0)
+    return jnp.concatenate(blocks, axis=d)
+
+
 def scaled_rows(widened, summed, gain_row):
     inverse = lax.rsqrt(summed / D + epsilon)
     return (widened * inverse * gain_row.astype(jnp.float32)).astype(jnp.bfloat16)
@@ -20,9 +27,7 @@
     partial_sum = jnp.sum(widened * widened, axis=1, keepdims=True)
     if which == 0:
         summed = lax.psum(partial_sum, "col")
-        return lax.all_gather(
-            scaled_rows(widened, summed, gain_row[None, :]), "col", axis=1, tiled=True
-        )
+        return all_by_exchange(scaled_rows(widened, summed, gain_row[None, :]), "col", 1)
     else:
         summed = lax.psum(partial_sum, "col")
         return lax.all_gather(

time: 447 us -> 387 us (0.87)
  waiting for transfers between devices: 329 us -> 261 us
  starting transfers between devices: 0.35 us -> 5.16 us
    all_gather x2 -> x1, waiting for transfers between devices: 116 us -> 57.3 us  [spread_norm(): lax.all_gather(scaled_rows(widened, summed, gain_row[None, :]), 'col', ax...]
    all_to_all x0 -> x1, waiting for transfers between devices: none -> 44.5 us  [all_by_exchange(): blocks = lax.all_to_all(blocks, axis, split_axis=0, concat_axis=0)]
    all_gather x1, waiting for transfers between devices: 37.4 us -> 0.02 us  [shards(): lax.all_gather(key_weight, 'row', axis=0, tiled=True)]
    all_gather x1, waiting for transfers between devices: 34.7 us -> 19.3 us  [shards(): lax.all_gather(value_weight, 'row', axis=0, tiled=True)]
    all_to_all x0 -> x1, starting transfers between devices: none -> 4.67 us  [all_by_exchange(): blocks = lax.all_to_all(blocks, axis, split_axis=0, concat_axis=0)]
  transfers between devices with their start and end apart: 9 -> 9, of which waited for: 9 -> 7; matrix products, arithmetic and copies ran while one was open for 7% -> 9% of each run, Pallas kernels for 0% -> 0%
where the time goes in v1:
time: 387 us
  waiting for transfers between devices  261 us (67%)
  blocking collectives  65.5 us (17%)
  matrix products  28.2 us (7%)
  between operations  14.2 us (4%)
  local copies, waits for them, and re-layouts  10.8 us (3%)
  starting transfers between devices  5.16 us (1%)
    psum x2, blocking collectives, spread_norm(): summed = lax.psum(partial_sum, 'col')  65.5 us
    all_gather x1, waiting for transfers between devices, shards(): heads_full = lax.all_gather(attended, 'col', axis=1, tiled=True)  61.3 us
    all_gather x1, waiting for transfers between devices, spread_norm(): lax.all_gather(scaled_rows(widened, summed, gain_row[None, :]), 'col', ax...  57.3 us
    all_to_all x1, waiting for transfers between devices, all_by_exchange(): blocks = lax.all_to_all(blocks, axis, split_axis=0, concat_axis=0)  44.5 us
    all_gather x1, waiting for transfers between devices, shards(): lax.all_gather(crossvalue_weight, 'row', axis=0, tiled=True)  36.7 us
    all_gather x1, waiting for transfers between devices, shards(): lax.all_gather(out_weight, 'row', axis=0, tiled=True)  33.8 us
    dot_general x6, matrix products, add_terms(): jnp.dot(source, weight_piece, preferred_element_type=jnp.float32)  26.5 us
    all_gather x1, waiting for transfers between devices, shards(): lax.all_gather(value_weight, 'row', axis=0, tiled=True)  19.3 us
  transfers between devices with their start and end apart: 9, of which 7 were waited for; matrix products, arithmetic and copies ran while one was open for 9% of the time, Pallas kernels for 0%

profile of v1, /device:TPU:1, one launch (start us, length us, event | category | flops | bytes accessed | tf_op | source)
XLA Modules:
  0.0 386.7 jit_solution(7643345845689641159)
XLA Ops:
  7.2 0.0 all-gather.11.cloned.1.call-start
  7.2 0.7 all-gather.11.cloned.1.call-update
  7.9 0.0 all-gather.13.cloned.1.call-start
  7.9 0.7 all-gather.13.cloned.1.call-update
  8.6 0.0 all-gather.9.cloned.1.call-start
  8.7 0.7 all-gather.9.cloned.1.call-update
  9.4 0.7 copy.23
  10.1 6.0 %gather_fusion = bf16[512,256]{1,0:T(8,128)(2,1)S(1)} fusion(bf16[16384,256]{1,0:T(8,128)(2,1)} %param.13, s32[1024]{0:T(1024)S(1)} %pad_clamp_fusion), kind=kCustom, calls=%fused_computation | custom fusion | bytes 526336 | tf_op jit(solution)/shard_map/jit(_take)/gather | solution.py:79
  16.1 0.1 copy.18
  16.3 0.7 copy.22
  16.9 0.7 convert_element_type.57
  17.6 0.1 fusion.10
  17.7 34.2 %psum.14 = f32[512,1]{0,1:T(1,128)S(1)} all-reduce(f32[512,1]{0,1:T(1,128)S(1)} %bitcast.51), channel_id=1, replica_groups=mesh['row'=16,'col'=16] {'col'}, use_global_device_ids=true, to_apply=%region_1.2 | all-reduce | flops 512 | bytes 4096 | tf_op jit(solution)/shard_map/psum | solution.py:29
  52.0 0.1 fusion.12
  52.1 2.4 stack.2
  54.5 0.0 copy-start
  54.5 4.7 %all-to-all-start = ((bf16[16,512,256]{1,2,0:T(8,128)(2,1)}), bf16[16,512,256]{1,2,0:T(8,128)(2,1)}, u32[]{:S(2)}, u32[]{:S(2)}) async-start(bf16[16,512,256]{1,2,0:T(8,128)(2,1)} %stack.2), calls=%async_computation | async-start | bytes 8388608 | tf_op jit(solution)/shard_map/all_to_all | solution.py:16
  59.1 0.0 all-gather.17.cloned.1.call-start
  59.2 0.5 all-gather.17.cloned.1.call-update
  59.7 0.0 all-gather.15.cloned.1.call-start
  59.8 0.0 copy-done
  59.8 0.1 iota_compare_fusion
  59.8 44.5 %all-to-all-done = bf16[16,512,256]{1,2,0:T(8,128)(2,1)} async-done(((bf16[16,512,256]{1,2,0:T(8,128)(2,1)}), bf16[16,512,256]{1,2,0:T(8,128)(2,1)}, u32[]{:S(2)}, u32[]{:S(2)}) %all-to-all-start) | async-done | bytes 4194336 | tf_op jit(solution)/shard_map/all_to_all | solution.py:16
  104.4 0.0 all-gather.11.cloned.1.call-done
  104.4 4.2 %convolution_convert_fusion.4 = bf16[512,256]{1,0:T(8,128)(2,1)S(1)} fusion(bf16[512,4096]{0,1:T(8,128)(2,1)} %bitcast.4, bf16[4096,256]{1,0:T(8,128)(2,1)} %all-gather.11.cloned.1.call-done), kind=kOutput, calls=%fused_computation.12 | convolution fusion | flops 1073872896 | bytes 6553600 | tf_op jit(solution)/shard_map/dot_general | solution.py:41
  108.6 0.0 all-gather.13.cloned.1.call-done
  108.6 4.2 %convolution_convert_fusion.3 = bf16[512,256]{1,0:T(8,128)(2,1)S(1)} fusion(bf16[512,4096]{0,1:T(8,128)(2,1)} %bitcast.4, bf16[4096,256]{1,0:T(8,128)(2,1)} %all-gather.13.cloned.1.call-done), kind=kOutput, calls=%fused_computation.11 | convolution fusion | flops 1073872896 | bytes 6553600 | tf_op jit(solution)/shard_map/dot_general | solution.py:41
  112.8 0.4 fusion.15
  113.2 0.3 fusion.3
  113.5 0.0 copy-start.1
  113.5 19.3 %all-gather.9.cloned.1.call-done = bf16[4096,256]{1,0:T(8,128)(2,1)} async-done(((bf16[256,256]{1,0:T(8,128)(2,1)}), bf16[4096,256]{1,0:T(8,128)(2,1)}) %all-gather.9.cloned.1.call-update) | async-done | bytes 2097168 | tf_op jit(solution)/shard_map/all_gather | solution.py:88
  132.8 4.2 %convolution_convert_fusion.5 = bf16[512,256]{1,0:T(8,128)(2,1)S(1)} fusion(bf16[512,4096]{0,1:T(8,128)(2,1)} %bitcast.4, bf16[4096,256]{1,0:T(8,128)(2,1)} %all-gather.9.cloned.1.call-done), kind=kOutput, calls=%fused_computation.13 | convolution fusion | flops 1073872896 | bytes 6553600 | tf_op jit(solution)/shard_map/dot_general | solution.py:41
  137.0 1.0 convolution_convert_fusion.2
  138.0 0.0 all-gather.15.cloned.1.call-update
  138.0 0.0 all-gather.21.cloned.1.call-start
  138.1 0.5 all-gather.21.cloned.1.call-update
  138.6 0.0 all-gather.19.cloned.1.call-start
  138.7 0.0 copy-done.1
  138.7 33.8 %all-gather.17.cloned.1.call-done = bf16[4096,256]{1,0:T(8,128)(2,1)} async-done(((bf16[256,256]{1,0:T(8,128)(2,1)}), bf16[4096,256]{1,0:T(8,128)(2,1)}) %all-gather.17.cloned.1.call-update) | async-done | bytes 2097168 | tf_op jit(solution)/shard_map/all_gather | solution.py:98
  172.5 61.3 %all-gather.15.cloned.1.call-done = bf16[512,4096]{1,0:T(8,128)(2,1)} async-done(((bf16[512,256]{1,0:T(8,128)(2,1)}), bf16[512,4096]{1,0:T(8,128)(2,1)}) %all-gather.15.cloned.1.call-update) | async-done | bytes 4194320 | tf_op jit(solution)/shard_map/all_gather | solution.py:97
  233.8 4.2 %fusion.7 = (f32[512]{0:T(512)S(1)}, bf16[512,256]{0,1:T(8,128)(2,1)S(1)}) fusion(bf16[512,4096]{1,0:T(8,128)(2,1)} %all-gather.15.cloned.1.call-done, bf16[4096,256]{1,0:T(8,128)(2,1)} %all-gather.17.cloned.1.call-done, bf16[512,256]{0,1:T(8,128)(2,1)S(1)} %copy.18, pred[512]{0:T(512)(128)(4,1)S(1)} %compare_and_fusion), kind=kOutput, calls=%fused_computation.20 | convolution fusion | flops 1074658816 | bytes 6818304 | tf_op jit(solution)/shard_map/dot_general | solution.py:41
  237.9 31.3 %psum.15 = f32[512,1]{0,1:T(1,128)S(1)} all-reduce(f32[512,1]{0,1:T(1,128)S(1)} %bitcast.57), channel_id=1, replica_groups=mesh['row'=16,'col'=16] {'col'}, use_global_device_ids=true, to_apply=%region_5.6 | all-reduce | flops 512 | bytes 4096 | tf_op jit(solution)/shard_map/psum | solution.py:32
  269.2 0.8 fusion.9
  270.0 0.0 all-gather.19.cloned.1.call-update
  270.1 0.2 all-gather.23.cloned.1.call-start
  270.3 0.5 all-gather.23.cloned.1.call-update
  270.8 0.8 copy.20
  271.7 4.4 %all-gather.21.cloned.1.call-done = bf16[4096,256]{1,0:T(8,128)(2,1)} async-done(((bf16[256,256]{1,0:T(8,128)(2,1)}), bf16[4096,256]{1,0:T(8,128)(2,1)}) %all-gather.21.cloned.1.call-update) | async-done | bytes 2097168 | tf_op jit(solution)/shard_map/all_gather | solution.py:104
  276.1 57.3 %all-gather.19.cloned.1.call-done = bf16[512,4096]{0,1:T(8,128)(2,1)} async-done(((bf16[512,256]{0,1:T(8,128)(2,1)}), bf16[512,4096]{0,1:T(8,128)(2,1)}) %all-gather.19.cloned.1.call-update) | async-done | bytes 4194320 | tf_op jit(solution)/shard_map/all_gather | solution.py:33
  333.4 4.9 %fusion.5 = bf16[512,1,256]{2,0,1:T(8,128)(2,1)} fusion(bf16[512,4096]{0,1:T(8,128)(2,1)} %all-gather.19.cloned.1.call-done, bf16[4096,256]{1,0:T(8,128)(2,1)} %all-gather.21.cloned.1.call-done), kind=kOutput, calls=%fused_computation.14 | convolution fusion | flops 1073872896 | bytes 6553600 | tf_op jit(solution)/shard_map/dot_general | solution.py:41
  338.2 36.7 %all-gather.23.cloned.1.call-done = bf16[4096,256]{1,0:T(8,128)(2,1)} async-done(((bf16[256,256]{1,0:T(8,128)(2,1)}), bf16[4096,256]{1,0:T(8,128)(2,1)}) %all-gather.23.cloned.1.call-update) | async-done | bytes 2097168 | tf_op jit(solution)/shard_map/all_gather | solution.py:105
  375.0 4.9 %fusion.6 = bf16[512,1,256]{2,0,1:T(8,128)(2,1)} fusion(bf16[512,4096]{0,1:T(8,128)(2,1)} %all-gather.19.cloned.1.call-done, bf16[4096,256]{1,0:T(8,128)(2,1)} %all-gather.23.cloned.1.call-done), kind=kOutput, calls=%fused_computation.15 | convolution fusion | flops 1073872896 | bytes 6553600 | tf_op jit(solution)/shard_map/dot_general | solution.py:41
  (6 shorter events, 0.0 us)
Async XLA Ops:
  7.2 97.2 %all-gather.11.cloned.1.call-start = ((), (), s32[]{:S(2)}) async-start(), calls=%async_computation.2 | async-start | bytes 2228224 | tf_op jit(solution)/shard_map/all_gather | solution.py:86
  7.9 100.7 %all-gather.13.cloned.1.call-start = ((), (), s32[]{:S(2)}) async-start(), calls=%async_computation.3 | async-start | bytes 2228224 | tf_op jit(solution)/shard_map/all_gather | solution.py:87
  8.6 124.2 %all-gather.9.cloned.1.call-start = ((), (), s32[]{:S(2)}) async-start(), calls=%async_computation.1 | async-start | bytes 2228224 | tf_op jit(solution)/shard_map/all_gather | solution.py:88
  54.5 5.3 %copy-start = (s32[2]{0:T(128)S(1)}, s32[2]{0:T(128)}, u32[]{:S(2)}) copy-start(s32[2]{0:T(128)} %param.12) | copy-start | bytes 28
  54.5 49.9 %all-to-all-start = ((bf16[16,512,256]{1,2,0:T(8,128)(2,1)}), bf16[16,512,256]{1,2,0:T(8,128)(2,1)}, u32[]{:S(2)}, u32[]{:S(2)}) async-start(bf16[16,512,256]{1,2,0:T(8,128)(2,1)} %stack.2), calls=%async_computation | async-start | bytes 8388608 | tf_op jit(solution)/shard_map/all_to_all | solution.py:16
  59.1 113.3 %all-gather.17.cloned.1.call-start = ((), (), s32[]{:S(2)}) async-start(), calls=%async_computation.5 | async-start | bytes 2228224 | tf_op jit(solution)/shard_map/all_gather | solution.py:98
  59.7 174.0 %all-gather.15.cloned.1.call-start = ((), (), s32[]{:S(2)}) async-start(), calls=%async_computation.4 | async-start | bytes 4456448 | tf_op jit(solution)/shard_map/all_gather | solution.py:97
  113.5 25.2 %copy-start.1 = (bf16[256]{0:T(256)(128)(2,1)S(1)}, bf16[256]{0:T(256)(128)(2,1)}, u32[]{:S(2)}) copy-start(bf16[256]{0:T(256)(128)(2,1)} %param.15) | copy-start | bytes 1540
  138.0 138.1 %all-gather.21.cloned.1.call-start = ((), (), s32[]{:S(2)}) async-start(), calls=%async_computation.7 | async-start | bytes 2228224 | tf_op jit(solution)/shard_map/all_gather | solution.py:104
  138.6 194.8 %all-gather.19.cloned.1.call-start = ((), (), s32[]{:S(2)}) async-start(), calls=%async_computation.6 | async-start | bytes 4456448 | tf_op jit(solution)/shard_map/all_gather | solution.py:33
  270.1 104.9 %all-gather.23.cloned.1.call-start = ((), (), s32[]{:S(2)}) async-start(), calls=%async_computation.8 | async-start | bytes 2228224 | tf_op jit(solution)/shard_map/all_gather | solution.py:105
Sparse Core Ops, SparseCore 0:
  9.8 43.6 all-gather.10
  55.3 37.6 all-gather.12
  94.8 37.9 all-gather.8
  134.5 37.9 all-gather.16
  175.3 58.4 all-gather.14
  235.4 40.6 all-gather.20
  279.1 54.2 all-gather.18
  335.2 39.7 all-gather.22
